TPU v7x, 32 devices: a whole 2x2x4 slice. The times are simulated.
32 devices in a mesh: scen: 8 (over z, x), row: 2 (over core), col: 2 (over y).
Axes of the slice: x: 2, y: 2, z: 4, core: 2. Of those that a mesh axis runs over, the one named last changes fastest.
Arguments:
- kkt: float32 [24, 768, 768], P('scen', ('row', 'col')), as said below
- border: float32 [24, 768, 4096], P('scen', None, ('row', 'col')), may hold values from -0.21875 to 0.21875
- first_diag: float32 [4096], P('scen'), may hold values from 0.5 to 1.5
- assignment: int32 [24], P('scen'), may hold values from 0 to 23, as said below
- panel: int32 [8], replicated, may hold values from 0 to 7, each once
Outputs:
- schur: float32 [4096, 4096], P('scen', ('row', 'col'))
- panel_factor: float32 [4096, 512], P('scen', ('row', 'col'))
Inputs may be any that keep to these rules, and one draw needn't show every extreme that they name: assignment is a permutation; with k = d * 3 + j (0 <= j < 3), assignment[k] is either k or (d XOR 1) * 3 + j, and the two scenarios of such a pair are either both fixed or swapped. panel is a permutation. Each kkt block is symmetric positive definite; after scaling by its diagonal, the off-diagonal part has spectral norm about one half.
All inputs are finite; a program needn't handle non-finite values.
Results may differ from a plain program's by a relative error of at most 0.00015.
Values sent between devices are 32-bit elements; how exact they have to be, the bound alone decides.
A program may use at most 192 MiB of HBM per device.

v0:
```python
import jax
import jax.numpy as jnp
from jax import lax
from jax.sharding import PartitionSpec as P

NK = 768
NF = 4096
PW = 512
NEWTON = 3


HIGH = lax.Precision.HIGHEST


def swapped(value, axis, distance):
    mask = 2**distance
    pairs = [(source, source ^ mask) for source in range(lax.axis_size(axis))]
    return lax.ppermute(value, axis, pairs)


def matmul(left, right):
    return jnp.dot(left, right, precision=HIGH, preferred_element_type=jnp.float32)


def contract(left, right):
    return lax.dot_general(
        left, right, (((0,), (0,)), ((), ())), precision=HIGH, preferred_element_type=jnp.float32
    )


def body(kkt, border, first_diag, assignment, panel):
    scen_index = lax.axis_index("scen")
    own_index = lax.axis_index(("row", "col"))
    slots = kkt.shape[0]
    partner = swapped(border, "scen", 0)
    kkt_all = lax.all_gather(kkt, ("row", "col"), axis=1, tiled=True)
    row_count = kkt.shape[1]
    col_count = border.shape[2]
    first_row = own_index * row_count
    row_ids = first_row + jnp.arange(row_count, dtype=jnp.int32)
    eye_rows = (jnp.arange(NK, dtype=jnp.int32)[None, :] == row_ids[:, None]).astype(jnp.float32)
    tile_total = jnp.zeros((NF, col_count), jnp.float32)
    for slot in range(slots):
        scenario_id = scen_index * slots + slot
        chosen = jnp.where(assignment[slot] == scenario_id, border[slot], partner[slot])
        kkt_rows = kkt[slot]
        kkt_full = kkt_all[slot]
        inv_diag = 1.0 / jnp.diagonal(kkt_full)
        local_inv = lax.dynamic_slice_in_dim(inv_diag, first_row, row_count)
        approx = (
            2.0 * (eye_rows * local_inv[:, None])
            - local_inv[:, None] * kkt_rows * inv_diag[None, :]
        )
        for step in range(NEWTON - 1):
            left = matmul(approx, kkt_full)

            def add_block(total, piece, start, left=left):
                return matmul(left, piece)

            product = add_block(
                jnp.zeros_like(approx),
                lax.all_gather(approx, ("row", "col"), axis=0, tiled=True),
                jnp.int32(0),
            )
            approx = 2.0 * approx - product

        def solve_piece(piece, start, chosen=chosen):
            return matmul(piece, chosen)

        solved = solve_piece(
            lax.all_gather(approx, ("row", "col"), axis=0, tiled=True), jnp.int32(0)
        )

        def border_piece(piece, start, solved=solved):
            return contract(piece, solved)

        tile = border_piece(
            lax.all_gather(chosen, ("row", "col"), axis=1, tiled=True), jnp.int32(0)
        )
        tile_total = tile_total + tile
    summed = lax.psum_scatter(tile_total, "scen", scatter_dimension=0, tiled=True)
    row_span = summed.shape[0]
    global_rows = scen_index * row_span + jnp.arange(row_span, dtype=jnp.int32)
    global_cols = own_index * col_count + jnp.arange(col_count, dtype=jnp.int32)
    on_diag = global_rows[:, None] == global_cols[None, :]
    schur = summed + jnp.where(on_diag, first_diag[:, None], 0.0)
    panel_start = panel[0] * PW
    panel_ids = panel_start + jnp.arange(PW, dtype=jnp.int32)
    select_cols = (global_cols[:, None] == panel_ids[None, :]).astype(jnp.float32)
    select_rows = (panel_ids[:, None] == global_rows[None, :]).astype(jnp.float32)
    panel_rows = lax.psum(matmul(schur, select_cols), ("row", "col"))
    block = lax.psum(matmul(select_rows, panel_rows), "scen")
    symmetric = 0.5 * (block + block.T)
    lower_factor = jnp.linalg.cholesky(symmetric)
    factor = lax.linalg.triangular_solve(
        lower_factor, panel_rows, left_side=False, lower=True, transpose_a=True
    )
    share = PW // lax.axis_size(("row", "col"))
    own_cols = lax.dynamic_slice_in_dim(factor, own_index * share, share, 1)
    return (schur, own_cols)


def solution(mesh):
    in_specs = (
        P("scen", ("row", "col"), None),
        P("scen", None, ("row", "col")),
        P("scen"),
        P("scen"),
        P(),
    )
    out_specs = (P("scen", ("row", "col")), P("scen", ("row", "col")))
    return jax.shard_map(body, mesh=mesh, in_specs=in_specs, out_specs=out_specs, check_vma=False)
```

profile of v0, /device:TPU:0, one launch (start us, length us, event | category | flops | bytes accessed | tf_op | source)
XLA Modules:
  0.0 1276.0 jit_solution(8011691956616219220)
XLA Ops:
  7.2 0.7 all-gather.17.cloned.1.call-update
  8.0 55.1 %all-gather.17.cloned.1.call-done = f32[3,768,768]{2,1,0:T(8,128)} async-done(((f32[3,192,768]{2,1,0:T(8,128)}), f32[3,768,768]{2,1,0:T(8,128)}) %all-gather.17.cloned.1.call-update) | async-done | bytes 7077904 | tf_op jit(solution)/shard_map/all_gather | solution.py:36
  63.1 5.7 slice_bitcast_fusion
  68.8 12.2 gather_fusion.1
  81.0 12.1 gather_fusion.2
  93.3 6.3 gather_fusion
  99.7 3.1 fusion.30
  104.1 3.5 fusion.27
  107.7 19.3 %all-gather.31.cloned.1.call-done = f32[768,768]{1,0:T(8,128)} async-done(((f32[192,768]{1,0:T(8,128)}), f32[768,768]{1,0:T(8,128)}) %all-gather.31.cloned.1.call-update) | async-done | bytes 2359312 | tf_op jit(solution)/shard_map/all_gather | solution.py:62
  127.0 4.3 convolution_subtract_fusion.1
  131.3 3.6 fusion.31
  134.9 17.8 %all-gather.25.cloned.1.call-done = f32[768,768]{1,0:T(8,128)} async-done(((f32[192,768]{1,0:T(8,128)}), f32[768,768]{1,0:T(8,128)}) %all-gather.25.cloned.1.call-update) | async-done | bytes 2359312 | tf_op jit(solution)/shard_map/all_gather | solution.py:62
  152.7 4.2 convolution_subtract_fusion.3
  157.2 3.5 fusion.35
  160.7 17.4 %all-gather.19.cloned.1.call-done = f32[768,768]{1,0:T(8,128)} async-done(((f32[192,768]{1,0:T(8,128)}), f32[768,768]{1,0:T(8,128)}) %all-gather.19.cloned.1.call-update) | async-done | bytes 2359312 | tf_op jit(solution)/shard_map/all_gather | solution.py:62
  178.1 4.2 convolution_subtract_fusion.5
  182.4 3.4 fusion.109
  185.8 17.8 %all-gather.33.cloned.1.call-done = f32[768,768]{1,0:T(8,128)} async-done(((f32[192,768]{1,0:T(8,128)}), f32[768,768]{1,0:T(8,128)}) %all-gather.33.cloned.1.call-update) | async-done | bytes 2359312 | tf_op jit(solution)/shard_map/all_gather | solution.py:62
  203.6 4.2 convolution_subtract_fusion
  207.9 1.5 collective-permute-start
  209.4 3.4 fusion.108
  212.9 16.2 %all-gather.27.cloned.1.call-done = f32[768,768]{1,0:T(8,128)} async-done(((f32[192,768]{1,0:T(8,128)}), f32[768,768]{1,0:T(8,128)}) %all-gather.27.cloned.1.call-update) | async-done | bytes 2359312 | tf_op jit(solution)/shard_map/all_gather | solution.py:62
  229.1 4.2 convolution_subtract_fusion.2
  233.8 3.4 fusion.107
  237.2 18.1 %all-gather.21.cloned.1.call-done = f32[768,768]{1,0:T(8,128)} async-done(((f32[192,768]{1,0:T(8,128)}), f32[768,768]{1,0:T(8,128)}) %all-gather.21.cloned.1.call-update) | async-done | bytes 2359312 | tf_op jit(solution)/shard_map/all_gather | solution.py:62
  255.3 4.2 convolution_subtract_fusion.4
  262.2 151.2 %collective-permute-done = f32[3,768,1024]{2,1,0:T(8,128)} collective-permute-done((f32[3,768,1024]{2,1,0:T(8,128)}, f32[3,768,1024]{2,1,0:T(8,128)}, u32[]{:S(2)}, u32[]{:S(2)}) %collective-permute-start) | collective-permute-done | bytes 9437216 | tf_op jit(solution)/shard_map/ppermute | solution.py:18
  413.3 11.1 slice_select_fusion
  425.1 0.7 all-gather.41.cloned.1.call-update
  425.9 1.1 copy-done
  426.9 10.4 fusion.8
  437.3 12.2 fusion.10
  449.6 10.4 fusion.12
  460.0 46.7 %all-gather.39.cloned.1.call-done = f32[1,768,4096]{2,1,0:T(8,128)} async-done(((f32[1,768,1024]{2,1,0:T(8,128)}), f32[1,768,4096]{2,1,0:T(8,128)}) %all-gather.39.cloned.1.call-update) | async-done | bytes 12582928 | tf_op jit(solution)/shard_map/all_gather | solution.py:78
  506.7 45.4 %fusion.2 = f32[4096,1024]{1,0:T(8,128)} fusion(f32[768,1024]{1,0:T(8,128)} %fusion.10, f32[1,768,4096]{2,1,0:T(8,128)} %all-gather.39.cloned.1.call-done), kind=kOutput, calls=%fused_computation.8 | convolution fusion | flops 38654705664 | bytes 32505856 | tf_op jit(solution)/shard_map/dot_general | solution.py:26
  552.2 38.1 %all-gather.37.cloned.1.call-done = f32[1,768,4096]{2,1,0:T(8,128)} async-done(((f32[1,768,1024]{2,1,0:T(8,128)}), f32[1,768,4096]{2,1,0:T(8,128)}) %all-gather.37.cloned.1.call-update) | async-done | bytes 12582928 | tf_op jit(solution)/shard_map/all_gather | solution.py:78
  590.2 45.5 %fusion.4 = f32[4096,1024]{1,0:T(8,128)} fusion(f32[768,1024]{1,0:T(8,128)} %fusion.12, f32[1,768,4096]{2,1,0:T(8,128)} %all-gather.37.cloned.1.call-done), kind=kOutput, calls=%fused_computation.10 | convolution fusion | flops 38654705664 | bytes 32505856 | tf_op jit(solution)/shard_map/dot_general | solution.py:26
  635.8 38.1 %all-gather.41.cloned.1.call-done = f32[1,768,4096]{2,1,0:T(8,128)} async-done(((f32[1,768,1024]{2,1,0:T(8,128)}), f32[1,768,4096]{2,1,0:T(8,128)}) %all-gather.41.cloned.1.call-update) | async-done | bytes 12582928 | tf_op jit(solution)/shard_map/all_gather | solution.py:78
  673.9 47.5 %add_add_fusion = f32[4096,1024]{1,0:T(8,128)} fusion(f32[4096,1024]{1,0:T(8,128)} %fusion.4, f32[4096,1024]{1,0:T(8,128)} %fusion.2, f32[768,1024]{1,0:T(8,128)S(1)} %copy-done.3, f32[1,768,4096]{2,1,0:T(8,128)} %all-gather.41.cloned.1.call-done), kind=kOutput, calls=%fused_computation.5 | convolution fusion | flops 38663094272 | bytes 66060288 | tf_op jit(solution)/shard_map/dot_general | solution.py:26
  722.2 279.8 %reduce-scatter.2.cloned.1.call-done = f32[512,1024]{1,0:T(8,128)} async-done(((f32[4096,1024]{1,0:T(8,128)}), f32[512,1024]{1,0:T(8,128)}) %reduce-scatter.2.cloned.1.call-update) | async-done | bytes 2097168 | tf_op jit(solution)/shard_map/reduce_scatter | solution.py:81
  1001.9 1.9 select_add_fusion
  1003.8 1.3 copy-done.12
  1005.1 3.0 fusion.14
  1008.4 35.3 %all-reduce.4.cloned.1.call-done = f32[512,512]{1,0:T(8,128)} async-done(((f32[512,512]{1,0:T(8,128)}), f32[512,512]{1,0:T(8,128)}) %all-reduce.4.cloned.1.call-update) | async-done | bytes 1048592 | tf_op jit(solution)/shard_map/psum | solution.py:91
  1043.7 3.4 fusion.20
  1047.1 78.9 %all-reduce.6.cloned.1.call-done = f32[512,512]{0,1:T(8,128)} async-done(((f32[512,512]{0,1:T(8,128)}), f32[512,512]{0,1:T(8,128)}) %all-reduce.6.cloned.1.call-update) | async-done | bytes 1048592 | tf_op jit(solution)/shard_map/psum | solution.py:92
  1126.0 1.6 copy.12
  1128.5 11.7 cholesky.104
  1140.4 9.8 custom-call.30
  1150.9 11.9 cholesky.217
  1163.4 0.7 compare_reduce_fusion.3
  1164.1 9.8 custom-call.31
  1174.6 11.7 cholesky.238
  1187.0 9.8 custom-call.32
  1197.5 11.9 cholesky.255
  1212.7 10.4 while.1
  1213.4 1.9 bitcast_dynamic-update-slice_fusion.2
  1216.0 1.9 bitcast_dynamic-update-slice_fusion.2
  1218.6 1.9 bitcast_dynamic-update-slice_fusion.2
  1221.2 1.9 bitcast_dynamic-update-slice_fusion.2
  1223.2 40.1 %custom-call.33 = f32[4,128,128]{1,2,0:T(8,128)S(1)} custom-call(f32[4,128,128]{2,1,0:T(8,128)} %get-tuple-element.9), custom_call_target="InvertDiagBlocksLowerTriangular" | custom-call | tf_op jit(solution)/shard_map/triangular_solve | solution.py:95
  1264.7 1.0 convolution_subtract_fusion.6
  1266.2 1.5 convolution_subtract_fusion.8
  1268.2 0.8 copy.14
  (112 shorter events, 15.0 us)
Async XLA Ops:
  7.2 56.0 %all-gather.17.cloned.1.call-start = ((), (), s32[]{:S(2)}) async-start(), calls=%async_computation.1 | async-start | bytes 8847360 | tf_op jit(solution)/shard_map/all_gather | solution.py:36
  7.9 119.1 %all-gather.31.cloned.1.call-start = ((), (), s32[]{:S(2)}) async-start(), calls=%async_computation.8 | async-start | bytes 2949120 | tf_op jit(solution)/shard_map/all_gather | solution.py:62
  99.6 4.5 copy-start.2
  102.8 49.9 %all-gather.25.cloned.1.call-start = ((), (), s32[]{:S(2)}) async-start(), calls=%async_computation.5 | async-start | bytes 2949120 | tf_op jit(solution)/shard_map/all_gather | solution.py:62
  102.8 24.2 %copy-start.9 = (f32[192,768]{1,0:T(8,128)S(1)}, f32[192,768]{1,0:T(8,128)}, u32[]{:S(2)}) copy-start(f32[192,768]{1,0:T(8,128)} %get-tuple-element.30) | copy-start | bytes 1769476
  103.5 74.6 %all-gather.19.cloned.1.call-start = ((), (), s32[]{:S(2)}) async-start(), calls=%async_computation.2 | async-start | bytes 2949120 | tf_op jit(solution)/shard_map/all_gather | solution.py:62
  104.1 99.5 %all-gather.33.cloned.1.call-start = ((), (), s32[]{:S(2)}) async-start(), calls=%async_computation.9 | async-start | bytes 2949120 | tf_op jit(solution)/shard_map/all_gather | solution.py:62
  131.3 21.4 %copy-start.8 = (f32[192,768]{1,0:T(8,128)S(1)}, f32[192,768]{1,0:T(8,128)}, u32[]{:S(2)}) copy-start(f32[192,768]{1,0:T(8,128)} %get-tuple-element.32) | copy-start | bytes 1769476
  131.3 97.8 %all-gather.27.cloned.1.call-start = ((), (), s32[]{:S(2)}) async-start(), calls=%async_computation.6 | async-start | bytes 2949120 | tf_op jit(solution)/shard_map/all_gather | solution.py:62
  156.9 21.2 %copy-start.7 = (f32[192,768]{1,0:T(8,128)S(1)}, f32[192,768]{1,0:T(8,128)}, u32[]{:S(2)}) copy-start(f32[192,768]{1,0:T(8,128)} %get-tuple-element.31) | copy-start | bytes 1769476
  156.9 98.4 %all-gather.21.cloned.1.call-start = ((), (), s32[]{:S(2)}) async-start(), calls=%async_computation.3 | async-start | bytes 2949120 | tf_op jit(solution)/shard_map/all_gather | solution.py:62
  160.7 21.7 %copy-start.5 = (f32[192,768]{1,0:T(8,128)S(1)}, f32[192,768]{1,0:T(8,128)}, u32[]{:S(2)}) copy-start(f32[192,768]{1,0:T(8,128)} %convolution_subtract_fusion.1) | copy-start | bytes 1769476
  182.4 243.5 %all-gather.35.cloned.1.call-start = ((), (), s32[]{:S(2)}) async-start(), calls=%async_computation.10 | async-start | bytes 2949120 | tf_op jit(solution)/shard_map/all_gather | solution.py:71
  185.8 23.6 %copy-start.4 = (f32[192,768]{1,0:T(8,128)S(1)}, f32[192,768]{1,0:T(8,128)}, u32[]{:S(2)}) copy-start(f32[192,768]{1,0:T(8,128)} %convolution_subtract_fusion.3) | copy-start | bytes 1769476
  207.9 229.5 %all-gather.29.cloned.1.call-start = ((), (), s32[]{:S(2)}) async-start(), calls=%async_computation.7 | async-start | bytes 2949120 | tf_op jit(solution)/shard_map/all_gather | solution.py:71
  207.9 205.4 %collective-permute-start = (f32[3,768,1024]{2,1,0:T(8,128)}, f32[3,768,1024]{2,1,0:T(8,128)}, u32[]{:S(2)}, u32[]{:S(2)}) collective-permute-start(f32[3,768,1024]{2,1,0:T(8,128)} %param.6), channel_id=1, source_target_pairs={{0,4},{4,0},{8,12},{12,8},{16,20},{20,16},{24,28},{28,24},{1,5},{5... | collective-permute-start | bytes 28311560 | tf_op jit(solution)/shard_map/ppermute | solution.py:18
  212.9 20.9 %copy-start.6 = (f32[192,768]{1,0:T(8,128)S(1)}, f32[192,768]{1,0:T(8,128)}, u32[]{:S(2)}) copy-start(f32[192,768]{1,0:T(8,128)} %convolution_subtract_fusion.5) | copy-start | bytes 1769476
  233.3 216.2 %all-gather.23.cloned.1.call-start = ((), (), s32[]{:S(2)}) async-start(), calls=%async_computation.4 | async-start | bytes 2949120 | tf_op jit(solution)/shard_map/all_gather | solution.py:71
  237.2 22.4 %copy-start.13 = (s32[3]{0:T(128)S(1)}, s32[3]{0:T(128)}, u32[]{:S(2)}) copy-start(s32[3]{0:T(128)} %param.8) | copy-start | bytes 40
  259.6 247.2 %all-gather.39.cloned.1.call-start = ((), (), s32[]{:S(2)}) async-start(), calls=%async_computation.15 | async-start | bytes 15728640 | tf_op jit(solution)/shard_map/all_gather | solution.py:78
  424.5 165.8 %all-gather.37.cloned.1.call-start = ((), (), s32[]{:S(2)}) async-start(), calls=%async_computation.14 | async-start | bytes 15728640 | tf_op jit(solution)/shard_map/all_gather | solution.py:78
  425.1 1.9 copy-start
  425.1 248.8 %all-gather.41.cloned.1.call-start = ((), (), s32[]{:S(2)}) async-start(), calls=%async_computation.16 | async-start | bytes 15728640 | tf_op jit(solution)/shard_map/all_gather | solution.py:78
  425.8 576.1 %reduce-scatter.2.cloned.1.call-start = ((), (), s32[]{:S(2)}) async-start(), calls=%async_computation.11 | async-start | bytes 18874368 | tf_op jit(solution)/shard_map/reduce_scatter | solution.py:81
  437.3 12.2 copy-start.1
  552.2 121.8 %copy-start.3 = (f32[768,1024]{1,0:T(8,128)S(1)}, f32[768,1024]{1,0:T(8,128)}, u32[]{:S(2)}) copy-start(f32[768,1024]{1,0:T(8,128)} %fusion.8) | copy-start | bytes 9437188
  721.4 0.7 copy-start.15
  721.4 280.5 %copy-start.14 = (f32[512]{0:T(512)S(1)}, f32[512]{0:T(512)}, u32[]{:S(2)}) copy-start(f32[512]{0:T(512)} %param.7) | copy-start | bytes 6148
  721.5 322.2 %all-reduce.4.cloned.1.call-start = ((), (), s32[]{:S(2)}) async-start(), calls=%async_computation.12 | async-start | bytes 2097152 | tf_op jit(solution)/shard_map/psum | solution.py:91
  1003.8 1.3 copy-start.12
  1008.2 117.9 %all-reduce.6.cloned.1.call-start = ((), (), s32[]{:S(2)}) async-start(), calls=%async_computation.13 | async-start | bytes 2097152 | tf_op jit(solution)/shard_map/psum | solution.py:92
  1126.0 1.7 copy-start.10
  1174.2 89.1 %copy-start.11 = (f32[512,512]{1,0:T(8,128)S(1)}, f32[512,512]{1,0:T(8,128)}, u32[]{:S(2)}) copy-start(f32[512,512]{1,0:T(8,128)} %all-reduce.4.cloned.1.call-done) | copy-start | bytes 3145732
Sparse Core Ops, SparseCore 0:
  9.5 53.5 all-gather.16
  102.9 24.0 all-gather.30
  128.5 24.0 all-gather.24
  154.1 23.9 all-gather.18
  179.5 24.0 all-gather.32
  205.0 24.0 all-gather.26
  231.2 24.0 all-gather.20
  256.9 24.0 all-gather.34
  282.5 24.0 all-gather.28
  308.6 24.0 all-gather.22
  424.6 82.0 all-gather.38
  508.1 82.0 all-gather.36
  591.8 82.0 all-gather.40
  721.6 280.2 reduce-scatter.1
  1008.3 35.3 all-reduce.3
  1047.2 78.7 all-reduce.5
where the time goes:
time: 1290 us; the launch traced here: 1280 us
  waiting for transfers between devices  833 us (65%)
  matrix products  231 us (18%)
  other arithmetic  136 us (11%)
  local copies, waits for them, and re-layouts  53.5 us (4%)
  between operations  19.3 us (1%)
    reduce_scatter x1, waiting for transfers between devices, body(): lax.psum_scatter(tile_total, 'scen', scatter_dimension=0, tiled=True)  280 us
    ppermute x1, waiting for transfers between devices, swapped(): return lax.ppermute(value, axis, pairs)  151 us
    dot_general x3, matrix products, contract(): lax.dot_general(left, right, (((0,), (0,)), ((), ())), precision=HIGH, pr...  138 us
    all_gather x3, waiting for transfers between devices, body(): lax.all_gather(chosen, ('row', 'col'), axis=1, tiled=True)  123 us
    all_gather x9, waiting for transfers between devices, body(): lax.all_gather(approx, ('row', 'col'), axis=0, tiled=True)  107 us
    dot_general x17, matrix products, matmul(): jnp.dot(left, right, precision=HIGH, preferred_element_type=jnp.float32)  85.6 us
    another operation x15, other arithmetic, body(): lower_factor = jnp.linalg.cholesky(symmetric)  79.5 us
    psum x1, waiting for transfers between devices, body(): block = lax.psum(matmul(select_rows, panel_rows), 'scen')  78.9 us
  transfers between devices with their start and end apart: 17, of which 14 were waited for; matrix products, arithmetic and copies ran while one was open for 14% of the time, Pallas kernels for 0%

commit v1 on v0

v1 whole, which is shorter than its diff:
```python
import jax
import jax.numpy as jnp
from jax import lax
from jax.sharding import PartitionSpec as P

PW = 512
NEWTON = 3


HIGH = lax.Precision.HIGH
GROUP = ("row", "col")


def swapped(value, axis, distance):
    mask = 2**distance
    pairs = [(source, source ^ mask) for source in range(lax.axis_size(axis))]
    return lax.ppermute(value, axis, pairs)


def gathered_rows(value, axis):
    count = lax.axis_size(axis)
    index = lax.axis_index(axis)
    rows = value.shape[1]
    whole = jnp.zeros((value.shape[0], rows * count, value.shape[2]), value.dtype)
    whole = lax.dynamic_update_slice_in_dim(whole, value, index * rows, 1)
    for shift in range(1, count):
        pairs = [(source, (source + shift) % count) for source in range(count)]
        origin = lax.rem(index - shift + count, count)
        whole = lax.dynamic_update_slice_in_dim(
            whole, lax.ppermute(value, axis, pairs), origin * rows, 1
        )
    return whole


def matmul(left, right, precision=HIGH):
    return jnp.dot(left, right, precision=precision, preferred_element_type=jnp.float32)


def contract(left, right):
    return lax.dot_general(
        left, right, (((0,), (0,)), ((), ())), precision=HIGH, preferred_element_type=jnp.float32
    )


def body(kkt, border, first_diag, assignment, panel):
    scen_index = lax.axis_index("scen")
    own_index = lax.axis_index(GROUP)
    group_size = lax.axis_size(GROUP)
    slots, order, col_count = border.shape
    width = col_count * group_size
    scenario_ids = scen_index * slots + jnp.arange(slots, dtype=jnp.int32)
    kkt = jnp.where((assignment == scenario_ids)[:, None, None], kkt, swapped(kkt, "scen", 0))
    kkt_all = gathered_rows(gathered_rows(kkt, "col"), "row")
    gathered = lax.all_gather(border, GROUP, axis=2, tiled=True)
    eye = jnp.eye(order, dtype=jnp.bool_)
    inverses = []
    for slot in range(slots):
        full = kkt_all[slot]
        diag = jnp.where(eye, full, 0.0)
        row_inv = 1.0 / jnp.sum(diag, axis=1, keepdims=True)
        col_inv = 1.0 / jnp.sum(diag, axis=0, keepdims=True)
        approx = jnp.where(eye, 2.0 * row_inv, 0.0) - row_inv * full * col_inv
        for step in range(NEWTON - 1):
            approx = 2.0 * approx - matmul(matmul(approx, full), approx)
        inverses.append(approx)
    solved = jnp.concatenate([matmul(inverses[slot], border[slot]) for slot in range(slots)], 0)
    border_all = gathered.reshape(slots * order, width)

    panel_start = panel[0] * PW
    share = PW // group_size
    own_start = panel_start + own_index * share

    share_solved = jnp.concatenate(
        [
            matmul(inverses[slot], lax.dynamic_slice_in_dim(gathered[slot], own_start, share, 1))
            for slot in range(slots)
        ],
        0,
    )
    panel_border = lax.dynamic_slice_in_dim(border_all, panel_start, PW, 1)
    block = contract(panel_border, share_solved)
    row_span = first_diag.shape[0]
    global_rows = scen_index * row_span + jnp.arange(row_span, dtype=jnp.int32)
    share_ids = own_start + jnp.arange(share, dtype=jnp.int32)
    owned = global_rows[:, None] == share_ids[None, :]
    share_diag = jnp.sum(jnp.where(owned, first_diag[:, None], 0.0), axis=0)
    panel_ids = panel_start + jnp.arange(PW, dtype=jnp.int32)
    block = block + jnp.where(panel_ids[:, None] == share_ids[None, :], share_diag[None, :], 0.0)
    block = lax.psum(block, "scen")
    block = lax.all_gather(block, GROUP, axis=1, tiled=True)
    symmetric = 0.5 * (block + block.T)
    lower_factor = jnp.linalg.cholesky(symmetric)
    lower_inverse = lax.linalg.triangular_solve(
        lower_factor, jnp.eye(PW, dtype=jnp.float32), left_side=True, lower=True
    )
    own_inverse = lax.dynamic_slice_in_dim(lower_inverse, own_index * share, share, 0)

    def schur_columns(start, count, solved):
        tile = contract(border_all, lax.dynamic_slice_in_dim(solved, start, count, 1))
        summed = lax.psum_scatter(tile, "scen", scatter_dimension=0, tiled=True)
        global_cols = own_index * col_count + start + jnp.arange(count, dtype=jnp.int32)
        on_diag = global_rows[:, None] == global_cols[None, :]
        return summed + jnp.where(on_diag, first_diag[:, None], 0.0)

    if col_count >= PW:
        pieces = col_count // PW
        first = lax.rem(panel[0], pieces)
        schur = jnp.zeros((row_span, col_count), jnp.float32)
        panel_rows = None
        for piece in range(pieces):
            start = lax.rem(first + piece, pieces) * PW
            columns = schur_columns(start, PW, solved)
            if piece == 0:
                owns = own_index == panel[0] // pieces
                columns, solved = lax.optimization_barrier((columns, solved))
                panel_rows = lax.psum(jnp.where(owns, columns, 0.0), GROUP)
            schur = lax.dynamic_update_slice_in_dim(schur, columns, start, 1)
    else:
        schur = schur_columns(jnp.int32(0), col_count, solved)
        parts = PW // col_count
        position = own_index - panel[0] * parts
        owns = (position >= 0) & (position < parts)
        placed = jnp.zeros((row_span, PW), jnp.float32)
        placed = lax.dynamic_update_slice_in_dim(
            placed, jnp.where(owns, schur, 0.0), jnp.clip(position, 0, parts - 1) * col_count, 1
        )
        panel_rows = lax.psum(placed, GROUP)
    own_cols = lax.dot_general(
        panel_rows,
        own_inverse,
        (((1,), (1,)), ((), ())),
        precision=lax.Precision.HIGHEST,
        preferred_element_type=jnp.float32,
    )
    return (schur, own_cols)


def solution(mesh):
    in_specs = (
        P("scen", ("row", "col"), None),
        P("scen", None, ("row", "col")),
        P("scen"),
        P("scen"),
        P(),
    )
    out_specs = (P("scen", ("row", "col")), P("scen", ("row", "col")))
    return jax.shard_map(body, mesh=mesh, in_specs=in_specs, out_specs=out_specs, check_vma=False)
```

time: 1290 us -> 762 us (0.59)
  waiting for transfers between devices: 833 us -> 382 us
  matrix products: 231 us -> 152 us
    all_gather x13 -> x2, waiting for transfers between devices: 285 us -> 66.7 us  [the longest x1 66.7 us: body(): gathered = lax.all_gather(border, GROUP, axis=2, tiled=True)]
    reduce_scatter x1 -> x2, waiting for transfers between devices: 280 us -> 160 us  [schur_columns(): summed = lax.psum_scatter(tile, 'scen', scatter_dimension=0, tiled=True)]
    ppermute x1, waiting for transfers between devices: 151 us -> 38.7 us  [swapped(): return lax.ppermute(value, axis, pairs)]
    ppermute x0 -> x2, waiting for transfers between devices: none -> 81.9 us  [gathered_rows(): lax.ppermute(value, axis, pairs)]
    psum x2, waiting for transfers between devices: 114 us -> 34.5 us  [the longest x1 34.5 us: body(): block = lax.psum(block, 'scen')]
    dot_general x3, matrix products: 138 us -> 78.2 us  [contract(): lax.dot_general(left, right, (((0,), (0,)), ((), ())), precision=HIGH, pr...]
    gather x3 -> x0, local copies, waits for them, and re-layouts: 30.6 us -> none  [body(): inv_diag = 1.0 / jnp.diagonal(kkt_full)]
    slice x1, local copies, waits for them, and re-layouts: 0.65 us -> 25.4 us  [body(): gathered[slot]]
  transfers between devices with their start and end apart: 17 -> 9, of which waited for: 14 -> 7; matrix products, arithmetic and copies ran while one was open for 14% -> 41% of each run, Pallas kernels for 0% -> 0%
where the time goes in v1:
time: 762 us; the launch traced here: 753 us
  waiting for transfers between devices  382 us (50%)
  matrix products  152 us (20%)
  other arithmetic  147 us (19%)
  local copies, waits for them, and re-layouts  48 us (6%)
  between operations  17.7 us (2%)
    reduce_scatter x2, waiting for transfers between devices, schur_columns(): summed = lax.psum_scatter(tile, 'scen', scatter_dimension=0, tiled=True)  160 us
    another operation x15, other arithmetic, body(): lower_factor = jnp.linalg.cholesky(symmetric)  86.3 us
    ppermute x2, waiting for transfers between devices, gathered_rows(): lax.ppermute(value, axis, pairs)  81.9 us
    dot_general x3, matrix products, contract(): lax.dot_general(left, right, (((0,), (0,)), ((), ())), precision=HIGH, pr...  78.2 us
    all_gather x1, waiting for transfers between devices, body(): gathered = lax.all_gather(border, GROUP, axis=2, tiled=True)  66.7 us
    dot_general x18, matrix products, matmul(): jnp.dot(left, right, precision=precision, preferred_element_type=jnp.floa...  63.4 us
    another operation x3, other arithmetic, body(): lax.linalg.triangular_solve(lower_factor, jnp.eye(PW, dtype=jnp.float32),...  40.8 us
    ppermute x1, waiting for transfers between devices, swapped(): return lax.ppermute(value, axis, pairs)  38.7 us
  transfers between devices with their start and end apart: 9, of which 7 were waited for; matrix products, arithmetic and copies ran while one was open for 41% of the time, Pallas kernels for 0%

profile of v1, /device:TPU:0, one launch (start us, length us, event | category | flops | bytes accessed | tf_op | source)
XLA Modules:
  0.0 752.9 jit_solution(10805813709153257614)
XLA Ops:
  8.6 3.0 collective-permute-start
  11.6 38.7 %collective-permute-done = f32[3,192,768]{2,1,0:T(8,128)} collective-permute-done((f32[3,192,768]{2,1,0:T(8,128)S(1)}, f32[3,192,768]{2,1,0:T(8,128)}, u32[]{:S(2)}, u32[]{:S(2)}) %collective-permute-start) | collective-permute-done | bytes 1769504 | tf_op jit(solution)/shard_map/ppermute | solution.py:17
  50.6 3.6 constant_dynamic-update-slice_fusion.5
  54.2 1.8 collective-permute-start.1
  56.0 77.4 %collective-permute-done.1 = f32[3,192,768]{2,1,0:T(8,128)} collective-permute-done((f32[3,192,768]{2,1,0:T(8,128)}, f32[3,192,768]{2,1,0:T(8,128)}, u32[]{:S(2)}, u32[]{:S(2)}) %collective-permute-start.1) | collective-permute-done | bytes 1769504 | tf_op jit(solution)/shard_map/ppermute | solution.py:30
  133.4 1.6 constant_dynamic-update-slice_fusion.4
  135.4 0.7 select_reduce_fusion
  137.0 4.5 collective-permute-done.2
  141.5 2.4 constant_dynamic-update-slice_fusion.2
  144.4 3.2 fusion.27
  147.6 3.6 multiply_subtract_fusion.5
  151.2 3.4 fusion.29
  154.6 3.2 multiply_subtract_fusion.4
  157.9 3.2 fusion.20
  161.1 3.5 multiply_subtract_fusion.3
  164.6 3.2 fusion.22
  167.9 3.1 multiply_subtract_fusion.2
  171.0 3.2 fusion.13
  174.3 3.5 multiply_subtract_fusion.1
  177.8 3.3 fusion.15
  181.1 3.1 multiply_subtract_fusion
  184.3 5.6 fusion.8
  189.9 5.6 fusion.6
  195.4 6.0 fusion.4
  201.4 9.4 %pad_maximum_fusion = f32[2304,1024]{1,0:T(8,128)} fusion(f32[768,1024]{1,0:T(8,128)} %fusion.4, f32[768,1024]{1,0:T(8,128)} %fusion.6, f32[768,1024]{1,0:T(8,128)} %fusion.8), kind=kLoop, calls=%fused_computation.2 | loop fusion | flops 4718592 | bytes 18874368 | tf_op jit(solution)/shard_map/concatenate | solution.py:66
  210.8 66.7 %all-gather.3.cloned.1.call-done = f32[3,768,4096]{2,1,0:T(8,128)} async-done(((f32[3,768,1024]{2,1,0:T(8,128)}), f32[3,768,4096]{2,1,0:T(8,128)}) %all-gather.3.cloned.1.call-update) | async-done | bytes 37748752 | tf_op jit(solution)/shard_map/all_gather | solution.py:54
  277.4 25.4 %fusion.157 = (f32[1,768,4096]{2,1,0:T(8,128)}, f32[1,768,4096]{2,1,0:T(8,128)}, f32[1,768,4096]{2,1,0:T(8,128)}) fusion(f32[3,768,4096]{2,1,0:T(8,128)} %all-gather.3.cloned.1.call-done), kind=kLoop, calls=%fused_computation.232 | loop fusion | bytes 75497472 | tf_op jit(solution)/shard_map/slice | solution.py:75
  302.8 2.2 fusion.109
  305.1 2.3 fusion.107
  307.3 2.1 fusion.105
  309.5 4.6 fusion.97
  314.3 36.4 %convolution_bitcast_fusion.1 = f32[4096,512]{1,0:T(8,128)} fusion(f32[2304,4096]{1,0:T(8,128)} %bitcast.165, f32[2304,1024]{1,0:T(8,128)} %pad_maximum_fusion, s32[]{:T(128)S(6)} %select_n.128), kind=kOutput, calls=%fused_computation.4 | convolution fusion | flops 28991029248 | bytes 50855940 | tf_op jit(solution)/shard_map/dot_general | solution.py:40
  350.8 34.5 %all-reduce.6.cloned.1.call-done = f32[512,128]{0,1:T(8,128)} async-done(((f32[512,128]{0,1:T(8,128)}), f32[512,128]{0,1:T(8,128)}) %all-reduce.6.cloned.1.call-update) | async-done | bytes 262160 | tf_op jit(solution)/shard_map/psum | solution.py:89
  385.5 150.2 %reduce-scatter.3.cloned.1.call-done = f32[512,512]{1,0:T(8,128)} async-done(((f32[4096,512]{1,0:T(8,128)}), f32[512,512]{1,0:T(8,128)}) %reduce-scatter.3.cloned.1.call-update) | async-done | bytes 1048592 | tf_op jit(solution)/shard_map/reduce_scatter | solution.py:100
  535.6 1.4 select_add_fusion
  537.3 1.2 broadcast_select_fusion.1
  538.5 1.3 copy-done.6
  540.1 37.2 %convolution_bitcast_fusion = f32[4096,512]{1,0:T(8,128)} fusion(f32[2304,4096]{1,0:T(8,128)} %bitcast.166, f32[2304,1024]{1,0:T(8,128)} %pad_maximum_fusion, s32[]{:T(128)S(6)} %select_n.130), kind=kOutput, calls=%fused_computation.3 | convolution fusion | flops 28991029248 | bytes 50855940 | tf_op jit(solution)/shard_map/dot_general | solution.py:40
  578.0 1.1 fusion.114
  579.2 1.7 copy.10
  581.7 11.7 %cholesky.103 = f32[128,128]{1,0:T(8,128)S(1)} custom-call(f32[128,128]{1,0:T(8,128)S(1)} %cholesky.263), custom_call_target="Cholesky" | custom-call | tf_op jit(solution)/shard_map/jit(cholesky)/cholesky | solution.py:92
  593.6 9.8 %custom-call.30 = f32[1,128,128]{1,2,0:T(8,128)S(1)} custom-call(f32[1,128,128]{2,1,0:T(8,128)S(1)} %get-tuple-element.46), custom_call_target="InvertDiagBlocksLowerTriangular" | custom-call | tf_op jit(solution)/shard_map/jit(cholesky)/cholesky | solution.py:92
  604.1 11.7 %cholesky.215 = f32[128,128]{1,0:T(8,128)S(1)} custom-call(f32[128,128]{1,0:T(8,128)S(1)} %cholesky.267), custom_call_target="Cholesky" | custom-call | tf_op jit(solution)/shard_map/jit(cholesky)/cholesky | solution.py:92
  616.4 10.0 %custom-call.31 = f32[1,128,128]{1,2,0:T(8,128)S(1)} custom-call(f32[1,128,128]{2,1,0:T(8,128)S(1)} %get-tuple-element.43), custom_call_target="InvertDiagBlocksLowerTriangular" | custom-call | tf_op jit(solution)/shard_map/jit(cholesky)/cholesky | solution.py:92
  627.6 13.2 %cholesky.236 = f32[128,128]{1,0:T(8,128)} custom-call(f32[128,128]{1,0:T(8,128)} %cholesky.272), custom_call_target="Cholesky" | custom-call | tf_op jit(solution)/shard_map/jit(cholesky)/cholesky | solution.py:92
  640.8 2.1 select_reduce_fusion.2
  642.9 11.3 %custom-call.32 = f32[1,128,128]{1,2,0:T(8,128)} custom-call(f32[1,128,128]{2,1,0:T(8,128)} %get-tuple-element.40), custom_call_target="InvertDiagBlocksLowerTriangular" | custom-call | tf_op jit(solution)/shard_map/jit(cholesky)/cholesky | solution.py:92
  654.2 1.0 convolution_dynamic-update-slice_fusion.1
  655.6 11.9 %cholesky.253 = f32[128,128]{1,0:T(8,128)S(1)} custom-call(f32[128,128]{1,0:T(8,128)S(1)} %convolution_subtract_fusion.5), custom_call_target="Cholesky" | custom-call | tf_op jit(solution)/shard_map/jit(cholesky)/cholesky | solution.py:92
  667.5 1.3 compare_reduce_fusion.2
  668.9 0.7 compare_reduce_fusion.3
  670.8 1.4 compare_reduce_fusion.1
  674.9 10.3 %while.1 = (s32[]{:T(128)}, f32[512,512]{1,0:T(8,128)S(1)}, s32[4,2]{0,1:T(2,128)S(1)}, f32[4,128,128]{2,1,0:T(8,128)}, s32[]{:T(128)}) while((s32[]{:T(128)}, f32[512,512]{1,0:T(8,128)S(1)}, s32[4,2]{0,1:T(2,128)S(1)}, f32[4,128,128]{2,1,0:T(8,128)}, s32[]{:T(128)}) %tuple.48), condition=%wide.while_cond, body=%wide.while_body.sunk | while | flops 2 | bytes 132705 | solution.py:93
  675.5 1.9 bitcast_dynamic-update-slice_fusion.2
  678.1 1.9 bitcast_dynamic-update-slice_fusion.2
  680.6 1.9 bitcast_dynamic-update-slice_fusion.2
  683.2 1.9 bitcast_dynamic-update-slice_fusion.2
  685.2 40.1 %custom-call.33 = f32[4,128,128]{1,2,0:T(8,128)S(1)} custom-call(f32[4,128,128]{2,1,0:T(8,128)} %get-tuple-element.13), custom_call_target="InvertDiagBlocksLowerTriangular" | custom-call | tf_op jit(solution)/shard_map/triangular_solve | solution.py:93
  726.9 1.3 fusion.131
  728.8 1.4 fusion.130
  730.3 3.0 fusion.118
  733.3 9.8 %reduce-scatter.5.cloned.1.call-done = f32[512,512]{1,0:T(8,128)} async-done(((f32[4096,512]{1,0:T(8,128)}), f32[512,512]{1,0:T(8,128)}) %reduce-scatter.5.cloned.1.call-update) | async-done | bytes 1048592 | tf_op jit(solution)/shard_map/reduce_scatter | solution.py:100
  743.0 1.4 add_dynamic-update-slice_fusion
  744.5 1.3 copy-done.8
  (100 shorter events, 14.8 us)
Async XLA Ops:
  7.2 1.5 copy-start.9
  7.2 4.4 copy-start.15
  7.2 270.2 %all-gather.3.cloned.1.call-start = ((), (), s32[]{:S(2)}) async-start(), calls=%async_computation.2 | async-start | bytes 47185920 | tf_op jit(solution)/shard_map/all_gather | solution.py:54
  7.9 377.4 %all-reduce.6.cloned.1.call-start = ((), (), s32[]{:S(2)}) async-start(), calls=%async_computation.6 | async-start | bytes 524288 | tf_op jit(solution)/shard_map/psum | solution.py:89
  8.6 41.7 %collective-permute-start = (f32[3,192,768]{2,1,0:T(8,128)S(1)}, f32[3,192,768]{2,1,0:T(8,128)}, u32[]{:S(2)}, u32[]{:S(2)}) collective-permute-start(f32[3,192,768]{2,1,0:T(8,128)S(1)} %copy-done.9), channel_id=1, source_target_pairs={{0,4},{4,0},{8,12},{12,8},{16,20},{20,16},{24,28},{28,24},{1,5},{5... | collective-permute-start | bytes 5308424 | tf_op jit(solution)/shard_map/ppermute | solution.py:17
  54.2 80.9 %copy-start.13 = (s32[8]{0:T(128)S(1)}, s32[8]{0:T(128)}, u32[]{:S(2)}) copy-start(s32[8]{0:T(128)} %param.9) | copy-start | bytes 100
  54.2 81.1 %copy-start.11 = (f32[512]{0:T(512)S(1)}, f32[512]{0:T(512)}, u32[]{:S(2)}) copy-start(f32[512]{0:T(512)} %param.7) | copy-start | bytes 6148
  54.2 79.2 %collective-permute-start.1 = (f32[3,192,768]{2,1,0:T(8,128)}, f32[3,192,768]{2,1,0:T(8,128)}, u32[]{:S(2)}, u32[]{:S(2)}) collective-permute-start(f32[3,192,768]{2,1,0:T(8,128)} %get-tuple-element.29), channel_id=1, source_target_pairs={{0,1},{1,0},{2,3},{3,2},{4,5},{5,4},{6,7},{7,6},{8,9},{9,8},{10,11... | collective-permute-start | bytes 5308424 | tf_op jit(solution)/shard_map/ppermute | solution.py:30
  135.1 6.4 collective-permute-start.2
  171.0 18.8 %copy-start = (f32[768,768]{1,0:T(8,128)}, f32[768,768]{1,0:T(8,128)S(1)}, u32[]{:S(2)}) copy-start(f32[768,768]{1,0:T(8,128)S(1)} %multiply_subtract_fusion.2) | copy-start | bytes 7077892
  174.2 10.0 %slice-start = ((s8[9437184]{0:T(1024)(128)(4,1)}), s8[4194304]{0:T(1024)(128)(4,1)S(1)}, s32[]{:S(2)}) async-start(s8[9437184]{0:T(1024)(128)(4,1)} %bitcast.167), calls=%async_computation.8 | async-start | bytes 8388608
  174.2 10.0 %slice-start.1 = ((s8[9437184]{0:T(1024)(128)(4,1)}), s8[4194304]{0:T(1024)(128)(4,1)S(1)}, s32[]{:S(2)}) async-start(s8[9437184]{0:T(1024)(128)(4,1)} %bitcast.167), calls=%async_computation.9 | async-start | bytes 8388608
  177.8 6.4 slice-start.2
  184.2 11.2 %copy-start.2 = (f32[768,768]{1,0:T(8,128)}, f32[768,768]{1,0:T(8,128)S(1)}, u32[]{:S(2)}) copy-start(f32[768,768]{1,0:T(8,128)S(1)} %multiply_subtract_fusion) | copy-start | bytes 7077892
  302.8 2.3 copy-start.1
  305.1 2.3 copy-start.3
  307.3 2.1 copy-start.12
  314.1 221.5 %reduce-scatter.3.cloned.1.call-start = ((), (), s32[]{:S(2)}) async-start(), calls=%async_computation.3 | async-start | bytes 9437184 | tf_op jit(solution)/shard_map/reduce_scatter | solution.py:100
  350.7 34.7 %copy-start.14 = (s32[8]{0:T(128)S(1)}, s32[8]{0:T(128)}, u32[]{:S(2)}) copy-start(s32[8]{0:T(128)} %param.9) | copy-start | bytes 100
  350.8 228.4 %all-gather.5.cloned.1.call-start = ((), (), s32[]{:S(2)}) async-start(), calls=%async_computation.7 | async-start | bytes 1310720 | tf_op jit(solution)/shard_map/all_gather | solution.py:90
  385.3 344.9 %all-reduce.4.cloned.1.call-start = ((), (), s32[]{:S(2)}) async-start(), calls=%async_computation.5 | async-start | bytes 2097152 | tf_op jit(solution)/shard_map/psum | solution.py:116
  538.5 1.3 copy-start.6
  539.9 203.1 %reduce-scatter.5.cloned.1.call-start = ((), (), s32[]{:S(2)}) async-start(), calls=%async_computation.4 | async-start | bytes 9437184 | tf_op jit(solution)/shard_map/reduce_scatter | solution.py:100
  579.2 1.7 copy-start.4
  626.6 99.0 %copy-start.5 = (f32[512,512]{1,0:T(8,128)S(1)}, f32[512,512]{1,0:T(8,128)}, u32[]{:S(2)}) copy-start(f32[512,512]{1,0:T(8,128)} %fusion.114) | copy-start | bytes 3145732
  725.3 0.7 copy-start.10
  728.8 14.2 %copy-start.7 = (f32[512,1024]{1,0:T(8,128)S(1)}, f32[512,1024]{1,0:T(8,128)}, u32[]{:S(2)}) copy-start(f32[512,1024]{1,0:T(8,128)} %copy-done.6) | copy-start | bytes 6291460
  744.5 1.3 copy-start.8
Sparse Core Ops, SparseCore 0:
  9.6 267.8 all-gather.2
  314.2 71.0 all-reduce.5
  388.9 146.6 reduce-scatter.2
  537.0 15.7 all-gather.4
  555.1 36.3 all-reduce.3
  594.9 148.0 reduce-scatter.4
